TPU v7x, 32 devices: a whole 2x2x4 slice. The times are simulated.
32 devices in a mesh: groups: 2 (over x), long: 16 (over z, y, core).
Axes of the slice: x: 2, y: 2, z: 4, core: 2. Of those that a mesh axis runs over, the one named last changes fastest.
Arguments:
- initial_state: float32 [2, 8192, 128], P(None, ('groups', 'long')), parts along dimension 1, may hold values from -6 to 6
- adjoint_state: float32 [2, 8192, 128], P(None, ('groups', 'long')), parts along dimension 1, may hold values from -6 to 6
- current_gates: float32 [8, 2, 128, 128], P('groups'), parts along dimension 0, may hold values from -0.375 to 0.375
Outputs:
- final_state: float32 [2, 8192, 128], P(None, ('groups', 'long')), parts along dimension 1
- final_adjoint: float32 [2, 8192, 128], P(None, ('groups', 'long')), parts along dimension 1
There are 2 independent parts, one for each index of `groups`. A program takes and returns all parts, laid end to end along the dimension named above; each array names one. Nothing has to cross between parts.
All inputs are finite; a program needn't handle non-finite values.
Results may differ from a plain program's by a relative error of at most 0.00017.
Values sent between devices are 32-bit elements; how exact they have to be, the bound alone decides.
A program may use at most 64 MiB of HBM per device.

v0:
```python
import jax
import jax.numpy as jnp
from jax import lax
from jax.sharding import PartitionSpec as P

SECTIONS = 4
NS_ITERS = 8


HIGHEST = lax.Precision.HIGHEST


def partner(x, axis, distance):
    return lax.ppermute(x, axis, [(i, i ^ 1 << distance) for i in range(lax.axis_size(axis))])


def matmul_high(left_side, right_side):
    return jnp.dot(left_side, right_side, precision=HIGHEST, preferred_element_type=jnp.float32)


def rows_product(left_side, right_side):
    return lax.dot_general(
        left_side,
        right_side,
        (((0,), (0,)), ((), ())),
        precision=HIGHEST,
        preferred_element_type=jnp.float32,
    )


def lanes_product(left_side, right_side):
    return lax.dot_general(
        left_side,
        right_side,
        (((1,), (1,)), ((), ())),
        precision=HIGHEST,
        preferred_element_type=jnp.float32,
    )


def polar_factor(summed_real, summed_imag, sweeps):
    norm_scale = lax.rsqrt(jnp.sum(summed_real * summed_real + summed_imag * summed_imag) + 1e-06)
    iterate_real = summed_real * norm_scale
    iterate_imag = summed_imag * norm_scale
    for sweep_index in range(sweeps):
        gram_real = rows_product(iterate_real, iterate_real) + rows_product(
            iterate_imag, iterate_imag
        )
        gram_imag = rows_product(iterate_real, iterate_imag) - rows_product(
            iterate_imag, iterate_real
        )
        product_real = matmul_high(iterate_real, gram_real) - matmul_high(iterate_imag, gram_imag)
        product_imag = matmul_high(iterate_real, gram_imag) + matmul_high(iterate_imag, gram_real)
        iterate_real = 1.5 * iterate_real - 0.5 * product_real
        iterate_imag = 1.5 * iterate_imag - 0.5 * product_imag
    return (iterate_real, iterate_imag)


def gate_rows(fields):
    count, rows, lanes = fields.shape
    viewed = fields.reshape(count, 2, rows // 2, 2, lanes // 2)
    return viewed.transpose(0, 2, 3, 1, 4).reshape(count, rows, lanes)


def slab_rows(fields):
    count, rows, lanes = fields.shape
    viewed = fields.reshape(count, rows // 2, 2, 2, lanes // 2)
    return viewed.transpose(0, 3, 1, 2, 4).reshape(count, rows, lanes)


def apply_lanes(field, gate_real, gate_imag):
    out_real = lanes_product(field[0], gate_real) - lanes_product(field[1], gate_imag)
    out_imag = lanes_product(field[0], gate_imag) + lanes_product(field[1], gate_real)
    return jnp.stack([out_real, out_imag])


def partial_environment(adjoint_field, state_field):
    outer_real = rows_product(adjoint_field[0], state_field[0]) + rows_product(
        adjoint_field[1], state_field[1]
    )
    outer_imag = rows_product(adjoint_field[1], state_field[0]) - rows_product(
        adjoint_field[0], state_field[1]
    )
    return (outer_real, outer_imag)


def split_pair(fields, is_lower):
    half_rows = fields.shape[1] // 2
    top_rows = fields[:, :half_rows]
    bottom_rows = fields[:, half_rows:]
    return (jnp.where(is_lower, top_rows, bottom_rows), jnp.where(is_lower, bottom_rows, top_rows))


def join_pair(kept_rows, received, is_lower):
    return jnp.concatenate(
        [jnp.where(is_lower, kept_rows, received), jnp.where(is_lower, received, kept_rows)], axis=1
    )


def shards(initial_state, adjoint_state, current_gates):
    bit_count = lax.axis_size("long").bit_length() - 1
    partner_bits = [bit_count - 1, bit_count // 2, 0, 1]
    device_index = lax.axis_index("long")
    state_now = initial_state
    adjoint_now = adjoint_state
    for section_index in range(SECTIONS):
        partner_bit = partner_bits[section_index % 4]
        is_lower = device_index // 2**partner_bit % 2 == 0
        old_real = current_gates[section_index, 0]
        old_imag = current_gates[section_index, 1]
        adjoint_kept, adjoint_sent = split_pair(adjoint_now, is_lower)
        adjoint_back = partner(adjoint_sent, "long", partner_bit)
        state_kept, state_sent = split_pair(state_now, is_lower)
        state_back = partner(state_sent, "long", partner_bit)
        state_in = gate_rows(join_pair(state_kept, state_back, is_lower))
        adjoint_out = apply_lanes(
            gate_rows(join_pair(adjoint_kept, adjoint_back, is_lower)), old_real, old_imag
        )
        part_real, part_imag = partial_environment(adjoint_out, state_in)
        summed_real, summed_imag = lax.psum((part_real, part_imag), "long")
        gate_real, gate_imag = polar_factor(summed_real, summed_imag, NS_ITERS)
        state_out = apply_lanes(state_in, gate_real, gate_imag)
        state_now = slab_rows(state_out)
        adjoint_now = slab_rows(adjoint_out)
    for back_index in range(SECTIONS - 1, -1, -1):
        partner_bit = partner_bits[back_index % 4]
        is_lower = device_index // 2**partner_bit % 2 == 0
        adjoint_kept, adjoint_sent = split_pair(adjoint_now, is_lower)
        adjoint_back = partner(adjoint_sent, "long", partner_bit)
        adjoint_now = join_pair(adjoint_kept, adjoint_back, is_lower)
    for back_index in range(SECTIONS - 1, -1, -1):
        partner_bit = partner_bits[back_index % 4]
        is_lower = device_index // 2**partner_bit % 2 == 0
        state_kept, state_sent = split_pair(state_now, is_lower)
        state_back = partner(state_sent, "long", partner_bit)
        state_now = join_pair(state_kept, state_back, is_lower)
    return (state_now, adjoint_now)


def solution(mesh):
    return jax.shard_map(
        shards,
        mesh=mesh,
        in_specs=(
            P(None, ("groups", "long"), None),
            P(None, ("groups", "long"), None),
            P("groups", None, None, None),
        ),
        out_specs=(P(None, ("groups", "long"), None), P(None, ("groups", "long"), None)),
        check_vma=False,
    )
```

profile of v0, /device:TPU:0, one launch (start us, length us, event | category | flops | bytes accessed | tf_op | source)
XLA Modules:
  0.0 537.8 jit_solution(13859174522461109207)
XLA Ops:
  7.2 1.0 fusion.264
  8.5 4.1 collective-permute-start.1
  12.9 0.9 collective-permute-start
  13.8 8.8 %collective-permute-done.1 = f32[2,128,128]{1,2,0:T(8,128)S(1)} collective-permute-done((f32[2,128,128]{1,2,0:T(8,128)S(1)}, f32[2,128,128]{1,2,0:T(8,128)S(1)}, u32[]{:S(2)}, u32[]{:S(2)}) %collective-permute-start.1) | collective-permute-done | bytes 131104 | tf_op jit(solution)/shard_map/ppermute | solution.py:14
  27.7 1.0 convolution_add_fusion.75
  28.7 1.0 convolution_subtract_fusion.75
  31.6 88.7 %all-reduce.15.cloned.1.call-done = (f32[128,128]{1,0:T(8,128)}, f32[128,128]{1,0:T(8,128)}) async-done(((f32[128,128]{1,0:T(8,128)}, f32[128,128]{1,0:T(8,128)}), (f32[128,128]{1,0:T(8,128)}, f32[128,128]{1,0:T(8,128)})) %all-reduce.15.cloned.1.call-update) | async-done | bytes 131088 | tf_op jit(solution)/shard_map/psum | solution.py:120
  120.3 1.5 add_reduce_fusion.3
  141.6 4.1 collective-permute-start.2
  151.5 1.0 convolution_add_fusion.58
  152.5 1.0 convolution_subtract_fusion.58
  156.9 83.8 %all-reduce.13.cloned.1.call-done = (f32[128,128]{1,0:T(8,128)}, f32[128,128]{1,0:T(8,128)}) async-done(((f32[128,128]{1,0:T(8,128)}, f32[128,128]{1,0:T(8,128)}), (f32[128,128]{1,0:T(8,128)}, f32[128,128]{1,0:T(8,128)})) %all-reduce.13.cloned.1.call-update) | async-done | bytes 131088 | tf_op jit(solution)/shard_map/psum | solution.py:120
  240.7 1.5 add_reduce_fusion.2
  265.4 1.0 convolution_add_fusion.41
  266.4 1.0 convolution_subtract_fusion.41
  270.2 89.6 %all-reduce.11.cloned.1.call-done = (f32[128,128]{1,0:T(8,128)}, f32[128,128]{1,0:T(8,128)}) async-done(((f32[128,128]{1,0:T(8,128)}, f32[128,128]{1,0:T(8,128)}), (f32[128,128]{1,0:T(8,128)}, f32[128,128]{1,0:T(8,128)})) %all-reduce.11.cloned.1.call-update) | async-done | bytes 131088 | tf_op jit(solution)/shard_map/psum | solution.py:120
  359.8 1.5 add_reduce_fusion.1
  381.1 0.9 collective-permute-start.6
  383.7 3.1 collective-permute-done.6
  388.5 1.0 convolution_add_fusion.24
  389.5 1.0 convolution_subtract_fusion.24
  391.2 88.9 %all-reduce.9.cloned.1.call-done = (f32[128,128]{1,0:T(8,128)}, f32[128,128]{1,0:T(8,128)}) async-done(((f32[128,128]{1,0:T(8,128)}, f32[128,128]{1,0:T(8,128)}), (f32[128,128]{1,0:T(8,128)}, f32[128,128]{1,0:T(8,128)})) %all-reduce.9.cloned.1.call-update) | async-done | bytes 131088 | tf_op jit(solution)/shard_map/psum | solution.py:120
  480.2 1.5 add_reduce_fusion
  502.8 4.6 collective-permute-done.8
  507.6 3.5 collective-permute-start.14
  511.1 1.3 collective-permute-start.10
  512.4 3.0 collective-permute-done.14
  515.5 1.5 collective-permute-start.15
  517.0 1.1 collective-permute-done.10
  518.1 1.5 collective-permute-start.11
  519.6 8.6 %collective-permute-done.15 = f32[2,128,128]{1,2,0:T(8,128)S(1)} collective-permute-done((f32[2,128,128]{1,2,0:T(8,128)S(1)}, f32[2,128,128]{1,2,0:T(8,128)S(1)}, u32[]{:S(2)}, u32[]{:S(2)}) %collective-permute-start.15) | collective-permute-done | bytes 131104 | tf_op jit(solution)/shard_map/ppermute | solution.py:14
  529.0 0.9 collective-permute-done.11
  (472 shorter events, 103.4 us)
Async XLA Ops:
  7.2 113.1 %all-reduce.15.cloned.1.call-start = ((), (), s32[]{:S(2)}) async-start(), calls=%async_computation.3 | async-start | bytes 262144 | tf_op jit(solution)/shard_map/psum | solution.py:120
  8.4 4.2 copy-start.9
  8.5 14.1 %collective-permute-start.1 = (f32[2,128,128]{1,2,0:T(8,128)S(1)}, f32[2,128,128]{1,2,0:T(8,128)S(1)}, u32[]{:S(2)}, u32[]{:S(2)}) collective-permute-start(f32[2,128,128]{1,2,0:T(8,128)S(1)} %broadcast_select_fusion.42), channel_id=1, source_target_pairs={{0,8},{1,9},{2,10},{3,11},{4,12},{5,13},{6,14},{7,15},{8,0},{9,1},... | collective-permute-start | bytes 393224 | tf_op jit(solution)/shard_map/ppermute | solution.py:14
  12.9 11.7 %collective-permute-start = (f32[2,128,128]{1,2,0:T(8,128)S(1)}, f32[2,128,128]{1,2,0:T(8,128)S(1)}, u32[]{:S(2)}, u32[]{:S(2)}) collective-permute-start(f32[2,128,128]{1,2,0:T(8,128)S(1)} %broadcast_select_fusion.46), channel_id=1, source_target_pairs={{0,8},{1,9},{2,10},{3,11},{4,12},{5,13},{6,14},{7,15},{8,0},{9,1},... | collective-permute-start | bytes 393224 | tf_op jit(solution)/shard_map/ppermute | solution.py:14
  22.8 1.0 copy-start.8
  30.5 210.2 %all-reduce.13.cloned.1.call-start = ((), (), s32[]{:S(2)}) async-start(), calls=%async_computation.2 | async-start | bytes 262144 | tf_op jit(solution)/shard_map/psum | solution.py:120
  30.8 114.9 %collective-permute-start.3 = (f32[2,128,128]{1,2,0:T(8,128)S(1)}, f32[2,128,128]{1,2,0:T(8,128)S(1)}, u32[]{:S(2)}, u32[]{:S(2)}) collective-permute-start(f32[2,128,128]{1,2,0:T(8,128)S(1)} %slice_select_fusion.12), channel_id=1, source_target_pairs={{0,4},{1,5},{2,6},{3,7},{4,0},{5,1},{6,2},{7,3},{8,12},{9,13},{10,... | collective-permute-start | bytes 393224 | tf_op jit(solution)/shard_map/ppermute | solution.py:14
  120.3 2.2 copy-start.1
  122.5 0.8 copy-start.5
  141.6 8.1 %collective-permute-start.2 = (f32[2,128,128]{1,2,0:T(8,128)S(1)}, f32[2,128,128]{1,2,0:T(8,128)S(1)}, u32[]{:S(2)}, u32[]{:S(2)}) collective-permute-start(f32[2,128,128]{1,2,0:T(8,128)S(1)} %slice_select_fusion.14), channel_id=1, source_target_pairs={{0,4},{1,5},{2,6},{3,7},{4,0},{5,1},{6,2},{7,3},{8,12},{9,13},{10,... | collective-permute-start | bytes 393224 | tf_op jit(solution)/shard_map/ppermute | solution.py:14
  149.6 4.0 collective-permute-start.5
  153.5 206.3 %all-reduce.11.cloned.1.call-start = ((), (), s32[]{:S(2)}) async-start(), calls=%async_computation.1 | async-start | bytes 262144 | tf_op jit(solution)/shard_map/psum | solution.py:120
  240.7 2.2 copy-start
  242.9 0.8 copy-start.4
  262.2 1.4 collective-permute-start.4
  262.5 5.8 %collective-permute-start.7 = (f32[2,128,128]{1,2,0:T(8,128)S(1)}, f32[2,128,128]{1,2,0:T(8,128)S(1)}, u32[]{:S(2)}, u32[]{:S(2)}) collective-permute-start(f32[2,128,128]{1,2,0:T(8,128)S(1)} %slice_select_fusion.4), channel_id=1, source_target_pairs={{0,2},{1,3},{2,0},{3,1},{4,6},{5,7},{6,4},{7,5},{8,10},{9,11},{10,... | collective-permute-start | bytes 393224 | tf_op jit(solution)/shard_map/ppermute | solution.py:14
  269.6 210.6 %all-reduce.9.cloned.1.call-start = ((), (), s32[]{:S(2)}) async-start(), calls=%async_computation | async-start | bytes 262144 | tf_op jit(solution)/shard_map/psum | solution.py:120
  359.8 2.2 copy-start.2
  362.0 0.8 copy-start.6
  381.1 5.7 %collective-permute-start.6 = (f32[2,128,128]{1,2,0:T(8,128)S(1)}, f32[2,128,128]{1,2,0:T(8,128)S(1)}, u32[]{:S(2)}, u32[]{:S(2)}) collective-permute-start(f32[2,128,128]{1,2,0:T(8,128)S(1)} %slice_select_fusion.6), channel_id=1, source_target_pairs={{0,2},{1,3},{2,0},{3,1},{4,6},{5,7},{6,4},{7,5},{8,10},{9,11},{10,... | collective-permute-start | bytes 393224 | tf_op jit(solution)/shard_map/ppermute | solution.py:14
  390.6 112.0 %collective-permute-start.12 = (f32[2,128,128]{1,2,0:T(8,128)S(1)}, f32[2,128,128]{1,2,0:T(8,128)S(1)}, u32[]{:S(2)}, u32[]{:S(2)}) collective-permute-start(f32[2,128,128]{1,2,0:T(8,128)S(1)} %slice_select_fusion), channel_id=1, source_target_pairs={{0,2},{1,3},{2,0},{3,1},{4,6},{5,7},{6,4},{7,5},{8,10},{9,11},{10,... | collective-permute-start | bytes 393224 | tf_op jit(solution)/shard_map/ppermute | solution.py:14
  480.2 2.2 copy-start.3
  482.4 0.8 copy-start.7
  501.7 5.7 %collective-permute-start.8 = (f32[2,128,128]{1,2,0:T(8,128)S(1)}, f32[2,128,128]{1,2,0:T(8,128)S(1)}, u32[]{:S(2)}, u32[]{:S(2)}) collective-permute-start(f32[2,128,128]{1,2,0:T(8,128)S(1)} %slice_select_fusion.2), channel_id=1, source_target_pairs={{0,2},{1,3},{2,0},{3,1},{4,6},{5,7},{6,4},{7,5},{8,10},{9,11},{10,... | collective-permute-start | bytes 393224 | tf_op jit(solution)/shard_map/ppermute | solution.py:14
  502.7 4.8 collective-permute-start.13
  507.4 3.7 collective-permute-start.9
  507.6 7.9 %collective-permute-start.14 = (f32[2,128,128]{1,2,0:T(8,128)S(1)}, f32[2,128,128]{1,2,0:T(8,128)S(1)}, u32[]{:S(2)}, u32[]{:S(2)}) collective-permute-start(f32[2,128,128]{1,2,0:T(8,128)S(1)} %get-tuple-element.15), channel_id=1, source_target_pairs={{0,4},{1,5},{2,6},{3,7},{4,0},{5,1},{6,2},{7,3},{8,12},{9,13},{10,... | collective-permute-start | bytes 393224 | tf_op jit(solution)/shard_map/ppermute | solution.py:14
  511.1 6.9 %collective-permute-start.10 = (f32[2,128,128]{1,2,0:T(8,128)S(1)}, f32[2,128,128]{1,2,0:T(8,128)S(1)}, u32[]{:S(2)}, u32[]{:S(2)}) collective-permute-start(f32[2,128,128]{1,2,0:T(8,128)S(1)} %get-tuple-element.24), channel_id=1, source_target_pairs={{0,4},{1,5},{2,6},{3,7},{4,0},{5,1},{6,2},{7,3},{8,12},{9,13},{10,... | collective-permute-start | bytes 393224 | tf_op jit(solution)/shard_map/ppermute | solution.py:14
  515.5 12.7 %collective-permute-start.15 = (f32[2,128,128]{1,2,0:T(8,128)S(1)}, f32[2,128,128]{1,2,0:T(8,128)S(1)}, u32[]{:S(2)}, u32[]{:S(2)}) collective-permute-start(f32[2,128,128]{1,2,0:T(8,128)S(1)} %get-tuple-element.12), channel_id=1, source_target_pairs={{0,8},{1,9},{2,10},{3,11},{4,12},{5,13},{6,14},{7,15},{8,0},{9,1},... | collective-permute-start | bytes 393224 | tf_op jit(solution)/shard_map/ppermute | solution.py:14
  518.1 11.9 %collective-permute-start.11 = (f32[2,128,128]{1,2,0:T(8,128)S(1)}, f32[2,128,128]{1,2,0:T(8,128)S(1)}, u32[]{:S(2)}, u32[]{:S(2)}) collective-permute-start(f32[2,128,128]{1,2,0:T(8,128)S(1)} %get-tuple-element.21), channel_id=1, source_target_pairs={{0,8},{1,9},{2,10},{3,11},{4,12},{5,13},{6,14},{7,15},{8,0},{9,1},... | collective-permute-start | bytes 393224 | tf_op jit(solution)/shard_map/ppermute | solution.py:14
Sparse Core Ops, SparseCore 0:
  30.7 89.5 all-reduce.14
  153.6 87.0 all-reduce.12
  269.7 90.0 all-reduce.10
  390.7 89.4 all-reduce.8
where the time goes:
time: 543 us; the launch traced here: 538 us
  waiting for transfers between devices  382 us (70%)
  matrix products  83.7 us (15%)
  starting transfers between devices  21.8 us (4%)
  local copies, waits for them, and re-layouts  20.6 us (4%)
  between operations  20.2 us (4%)
  other arithmetic  9.1 us (2%)
    psum x4, waiting for transfers between devices, shards(): summed_real, summed_imag = lax.psum((part_real, part_imag), 'long')  351 us
    dot_general x144, matrix products, rows_product(): lax.dot_general(left_side, right_side, (((0,), (0,)), ((), ())), precisio...  47.6 us
    ppermute x16, waiting for transfers between devices, partner(): lax.ppermute(x, axis, [(i, i ^ 1 << distance) for i in range(lax.axis_siz...  31.4 us
    dot_general x128, matrix products, matmul_high(): jnp.dot(left_side, right_side, precision=HIGHEST, preferred_element_type=...  26.5 us
    ppermute x16, starting transfers between devices, partner(): lax.ppermute(x, axis, [(i, i ^ 1 << distance) for i in range(lax.axis_siz...  21.5 us
  transfers between devices with their start and end apart: 20, of which 14 were waited for; matrix products, arithmetic and copies ran while one was open for 11% of the time, Pallas kernels for 0%

commit v1 on v0

v1 whole, which is shorter than its diff:
```python
import functools

import jax
import jax.numpy as jnp
from jax import lax
from jax.experimental import pallas as pl
from jax.experimental.pallas import tpu as pltpu
from jax.sharding import PartitionSpec as P

SECTIONS = 4
NS_ITERS = 8
MESH = pl.DeviceIdType.MESH
ADJ_IN, PSI_IN, RS, AG, MID, ADJ_OUT, PSI_OUT = 0, 1, 2, 6, 10, 14, 15


def split(x):
    high = x.astype(jnp.bfloat16)
    return high, (x - high.astype(jnp.float32)).astype(jnp.bfloat16)


def dot3(left, right, contract):
    def dot(a, b):
        return lax.dot_general(
            a, b, (contract, ((), ())), preferred_element_type=jnp.float32
        )

    return dot(left[0], right[0]) + (dot(left[0], right[1]) + dot(left[1], right[0]))


def embed_out(real, imag):
    return jnp.concatenate(
        [
            jnp.concatenate([real, -imag], axis=1),
            jnp.concatenate([imag, real], axis=1),
        ],
        axis=0,
    )


def swap_plane(plane, q, per):
    rows, lanes = plane.shape
    stride = per << q
    rolled = pltpu.roll(plane, lanes // 2, 1)
    low = lax.broadcasted_iota(jnp.int32, (stride, lanes), 1) < lanes // 2
    blocks = []
    for start in range(0, rows, 2 * stride):
        mid, end = start + stride, start + 2 * stride
        blocks.append(jnp.where(low, plane[start:mid], rolled[mid:end]))
        blocks.append(jnp.where(low, rolled[start:mid], plane[mid:end]))
    return jnp.concatenate(blocks, axis=0)


def swap(x, q, per):
    lanes = x.shape[1] // 2
    return jnp.concatenate(
        [swap_plane(x[:, :lanes], q, per), swap_plane(x[:, lanes:], q, per)], axis=1
    )


def polar(x, sweeps):
    gate = x.shape[0]
    norm = lax.rsqrt(jnp.sum(x * x, keepdims=True) + 1e-06)

    def sweep(_, a):
        high, low = split(a)

        def embed(v):
            real, imag = v[:, :gate], v[:, gate:]
            return jnp.concatenate([v, jnp.concatenate([-imag, real], axis=1)], axis=0)

        full = (embed(high), embed(low))
        gram = dot3((high, low), full, ((1,), (1,)))
        return 1.5 * a - 0.5 * dot3(split(gram), full, ((1,), (0,)))

    return lax.fori_loop(0, sweeps, sweep, x * norm)


def kernel(
    used, order, extra_bits,
    psi_in, adj_in, gates_in, psi_out, adj_out,
    psi_buf, adj_buf, gates, phi_t, psi_send, adj_send,
    part, rs_buf, ag_buf, mid_buf,
    send_sem, recv_sem, local_sem,
):
    group = lax.axis_index("groups")
    me = lax.axis_index("long")
    n = 2 ** len(used)
    extra = 2 ** len(extra_bits)
    rows = psi_in.shape[1]
    gate = psi_in.shape[2]
    per = rows // n
    own = gate // n

    def gather(value, bits):
        out = 0
        for k, bit in enumerate(bits):
            out = out + lax.rem(lax.div(value, 2**bit), 2) * 2**k
        return out

    def scatter(value, bits):
        out = 0
        for k, bit in enumerate(bits):
            out = out + lax.rem(lax.div(value, 2**k), 2) * 2**bit
        return out

    slot = gather(me, used)
    layer = gather(me, extra_bits)

    def peer(j):
        return scatter(j, used) + scatter(layer, extra_bits)

    def layer_peer(j):
        return scatter(slot, used) + scatter(j, extra_bits)

    def others(fn, mine=slot, count=n):
        def step(off, carry):
            fn(lax.rem(mine + off, count))
            return carry

        lax.fori_loop(1, count, step, 0)

    def remote(src, dst, phase, there, here, target):
        return pltpu.make_async_remote_copy(
            src_ref=src,
            dst_ref=dst,
            send_sem=send_sem.at[phase, there],
            recv_sem=recv_sem.at[phase, here],
            device_id={"groups": group, "long": target},
            device_id_type=MESH,
        )

    def block(ref, j, size):
        return ref.at[:, pl.ds(pl.multiple_of(j * size, size), size), :]

    def send_all(src, dst, phase, size):
        others(lambda j: remote(block(src, j, size), block(dst, slot, size), phase, j, slot, peer(j)).start())

    def recv_all(dst, phase, size):
        others(lambda j: remote(block(dst, j, size), block(dst, j, size), phase, j, j, peer(j)).wait_recv())

    def sent_all(src, phase, size):
        others(lambda j: remote(block(src, j, size), block(src, j, size), phase, j, j, peer(j)).wait_send())

    gate_copy = pltpu.make_async_copy(gates_in, gates, local_sem.at[0])
    adj_own = pltpu.make_async_copy(block(adj_in, slot, per), block(adj_buf, slot, per), local_sem.at[1])
    psi_own = pltpu.make_async_copy(block(psi_in, slot, per), block(psi_buf, slot, per), local_sem.at[2])
    adj_own.start()
    gate_copy.start()
    psi_own.start()

    barrier = pltpu.get_barrier_semaphore()
    others(lambda j: pl.semaphore_signal(barrier, inc=1, device_id={"groups": group, "long": peer(j)}, device_id_type=MESH))
    if extra > 1:
        others(
            lambda j: pl.semaphore_signal(barrier, inc=1, device_id={"groups": group, "long": layer_peer(j)}, device_id_type=MESH),
            layer, extra,
        )
    pl.semaphore_wait(barrier, n + extra - 2)

    send_all(adj_in, adj_buf, ADJ_IN, per)
    send_all(psi_in, psi_buf, PSI_IN, per)

    def joined(ref):
        return jnp.concatenate([ref[0], ref[1]], axis=1)

    def advance_adjoint(phi, s):
        full = split(embed_out(gates[s, 0], gates[s, 1]))
        phi = dot3(split(phi), full, ((1,), (1,)))
        high, low = split(phi.T)
        phi_t[0] = high
        phi_t[1] = low
        return phi

    gate_copy.wait()
    adj_own.wait()
    recv_all(adj_buf, ADJ_IN, per)
    phi = advance_adjoint(swap(joined(adj_buf), order[0], per), 0)
    psi_own.wait()
    recv_all(psi_buf, PSI_IN, per)
    psi = swap(joined(psi_buf), order[0], per)

    for s in range(SECTIONS):
        state = split(psi)
        outer = dot3((phi_t[0], phi_t[1]), state, ((1,), (0,)))
        part[s, 0] = outer[:gate, :gate] + outer[gate:, gate:]
        part[s, 1] = outer[gate:, :gate] - outer[:gate, gate:]
        others(
            lambda j: remote(block(part.at[s], j, own), rs_buf.at[s, slot], RS + s, j, slot, peer(j)).start()
        )
        if s + 1 < SECTIONS:
            phi = advance_adjoint(swap(phi, order[s + 1], per), s + 1)
        others(
            lambda j: remote(rs_buf.at[s, j], rs_buf.at[s, j], RS + s, j, j, peer(j)).wait_recv()
        )
        mine = pl.ds(pl.multiple_of(slot * own, own), own)
        rs_buf[s, slot] = part[s, :, mine, :]
        total = rs_buf[s, 0]
        for j in range(1, n):
            total = total + rs_buf[s, j]
        if extra > 1:
            mid_buf[s, layer] = total
            others(
                lambda j: remote(mid_buf.at[s, layer], mid_buf.at[s, layer], MID + s, j, layer, layer_peer(j)).start(),
                layer, extra,
            )
            others(
                lambda j: remote(mid_buf.at[s, j], mid_buf.at[s, j], MID + s, j, j, layer_peer(j)).wait_recv(),
                layer, extra,
            )
            total = mid_buf[s, 0]
            for j in range(1, extra):
                total = total + mid_buf[s, j]
        ag_buf[s, :, mine, :] = total
        held = block(ag_buf.at[s], slot, own)
        others(lambda j: remote(held, held, AG + s, j, slot, peer(j)).start())
        if s + 2 == SECTIONS:
            back = phi
            for q in order[::-1]:
                back = swap(back, q, per)
            adj_send[0] = back[:, :gate]
            adj_send[1] = back[:, gate:]
        recv_all(ag_buf.at[s], AG + s, own)
        if s + 2 == SECTIONS:
            send_all(adj_send, adj_out, ADJ_OUT, per)
        fitted = polar(jnp.concatenate([ag_buf[s, 0], ag_buf[s, 1]], axis=1), NS_ITERS)
        full = split(embed_out(fitted[:, :gate], fitted[:, gate:]))
        psi = dot3(state, full, ((1,), (1,)))
        if s + 1 < SECTIONS:
            psi = swap(psi, order[s + 1], per)

    for q in order[::-1]:
        psi = swap(psi, q, per)
    psi_send[0] = psi[:, :gate]
    psi_send[1] = psi[:, gate:]
    send_all(psi_send, psi_out, PSI_OUT, per)
    psi_back = pltpu.make_async_copy(block(psi_send, slot, per), block(psi_out, slot, per), local_sem.at[2])
    adj_back = pltpu.make_async_copy(block(adj_send, slot, per), block(adj_out, slot, per), local_sem.at[1])
    psi_back.start()
    adj_back.start()
    sent_all(adj_in, ADJ_IN, per)
    sent_all(psi_in, PSI_IN, per)
    for s in range(SECTIONS):
        sent_all(part.at[s], RS + s, own)
        sent_all(ag_buf.at[s], AG + s, own)
        if extra > 1:
            others(
                lambda j: remote(mid_buf.at[s, layer], mid_buf.at[s, layer], MID + s, j, j, layer_peer(j)).wait_send(),
                layer, extra,
            )
    sent_all(adj_send, ADJ_OUT, per)
    recv_all(adj_out, ADJ_OUT, per)
    adj_back.wait()
    psi_back.wait()
    sent_all(psi_send, PSI_OUT, per)
    recv_all(psi_out, PSI_OUT, per)


def shards(initial_state, adjoint_state, current_gates):
    bit_count = lax.axis_size("long").bit_length() - 1
    partner_bits = [bit_count - 1, bit_count // 2, 0, 1]
    used = sorted(set(partner_bits))
    assert len(used) == SECTIONS
    order = [used.index(bit) for bit in partner_bits]
    extra_bits = [bit for bit in range(bit_count) if bit not in used]
    n, extra = 2 ** len(used), 2 ** len(extra_bits)
    planes, rows, gate = initial_state.shape
    own = gate // n
    f32, bf16 = jnp.float32, jnp.bfloat16
    anywhere = pl.BlockSpec(memory_space=pl.ANY)
    return tuple(
        pl.pallas_call(
            functools.partial(kernel, used, order, extra_bits),
            out_shape=[jax.ShapeDtypeStruct(initial_state.shape, f32)] * 2,
            in_specs=[anywhere] * 3,
            out_specs=[anywhere] * 2,
            scratch_shapes=[
                pltpu.VMEM((2, rows, gate), f32),
                pltpu.VMEM((2, rows, gate), f32),
                pltpu.VMEM(current_gates.shape, f32),
                pltpu.VMEM((2, 2 * gate, rows), bf16),
                pltpu.VMEM((2, rows, gate), f32),
                pltpu.VMEM((2, rows, gate), f32),
                pltpu.VMEM((SECTIONS, 2, gate, gate), f32),
                pltpu.VMEM((SECTIONS, n, 2, own, gate), f32),
                pltpu.VMEM((SECTIONS, 2, gate, gate), f32),
                pltpu.VMEM((SECTIONS, extra, 2, own, gate), f32),
                pltpu.SemaphoreType.DMA((16, max(n, extra))),
                pltpu.SemaphoreType.DMA((16, max(n, extra))),
                pltpu.SemaphoreType.DMA((3,)),
            ],
            compiler_params=pltpu.CompilerParams(collective_id=0, has_side_effects=True),
            name="sweep",
        )(initial_state, adjoint_state, current_gates)
    )


def solution(mesh):
    return jax.shard_map(
        shards,
        mesh=mesh,
        in_specs=(
            P(None, ("groups", "long"), None),
            P(None, ("groups", "long"), None),
            P("groups", None, None, None),
        ),
        out_specs=(P(None, ("groups", "long"), None), P(None, ("groups", "long"), None)),
        check_vma=False,
    )
```

time: 543 us -> 94 us (0.17)
  waiting for transfers between devices: 382 us -> 0 us
  Pallas kernels: 0 us -> 90.3 us
  matrix products: 83.7 us -> 0 us
  starting transfers between devices: 21.8 us -> 0 us
  between operations: 20.2 us -> 0.65 us
  local copies, waits for them, and re-layouts: 20.6 us -> 2.42 us
  other arithmetic: 9.1 us -> 0 us
    psum x4 -> x0, waiting for transfers between devices: 351 us -> none  [shards(): summed_real, summed_imag = lax.psum((part_real, part_imag), 'long')]
    pallas_call x0 -> x1, Pallas kernels: none -> 90.3 us  [shards(): pl.pallas_call(functools.partial(kernel, used, order, extra_bits), out_sh...]
    dot_general x304 -> x0, matrix products: 83.7 us -> none  [the longest x144 47.6 us: rows_product(): lax.dot_general(left_side, right_side, (((0,), (0,)), ((), ())), precisio...]
    ppermute x16 -> x0, waiting for transfers between devices: 31.4 us -> none  [partner(): lax.ppermute(x, axis, [(i, i ^ 1 << distance) for i in range(lax.axis_siz...]
    ppermute x16 -> x0, starting transfers between devices: 21.5 us -> none  [partner(): lax.ppermute(x, axis, [(i, i ^ 1 << distance) for i in range(lax.axis_siz...]
    reduce_sum x4 -> x0, other arithmetic: 6.13 us -> none  [polar_factor(): jnp.sum(summed_real * summed_real + summed_imag * summed_imag) + 1e-06]
  transfers between devices with their start and end apart: 20 -> 0, of which waited for: 14 -> 0; matrix products, arithmetic and copies ran while one was open for 11% -> 0% of each run, Pallas kernels for 0% -> 0%
where the time goes in v1:
time: 94 us; the launch traced here: 93.3 us
  Pallas kernels  90.3 us (96%)
  local copies, waits for them, and re-layouts  2.42 us (3%)
    pallas_call x1, Pallas kernels, shards(): pl.pallas_call(functools.partial(kernel, used, order, extra_bits), out_sh...  90.3 us
    unnamed x4, local copies, waits for them, and re-layouts  2.42 us

profile of v1, /device:TPU:0, one launch (start us, length us, event | category | flops | bytes accessed | tf_op | source)
XLA Modules:
  0.0 93.3 jit_solution(1765497399919915784)
XLA Ops:
  0.6 90.3 %sweep.1 = (f32[2,256,128]{2,1,0:T(8,128)}, f32[2,256,128]{2,1,0:T(8,128)}) custom-call(f32[2,256,128]{2,1,0:T(8,128)} %psi_in.1, f32[2,256,128]{2,1,0:T(8,128)} %adj_in.1, f32[4,2,128,128]{3,2,1,0:T(8,128)} %gates_in.1), custom_call_target="tpu_custom_call" | custom-call | tf_op jit(solution)/shard_map/sweep/pallas_call | solution.py:271
  90.9 0.0 copy-start
  90.9 1.7 %copy.7 = f32[2,256,128]{2,1,0:T(8,128)} copy(f32[2,256,128]{2,1,0:T(8,128)} %get-tuple-element.4) | data formatting | bytes 524288
  92.6 0.0 copy-done
  92.6 0.7 copy.8
Async XLA Ops:
  90.9 1.7 %copy-start = (f32[2,256,128]{2,1,0:T(8,128)S(1)}, f32[2,256,128]{2,1,0:T(8,128)}, u32[]{:S(2)}) copy-start(f32[2,256,128]{2,1,0:T(8,128)} %get-tuple-element.5) | copy-start | bytes 786436

commit v2 on v1

--- a/solution.py
+++ b/solution.py
@@ -89,7 +89,9 @@
     rows = psi_in.shape[1]
     gate = psi_in.shape[2]
     per = rows // n
-    own = gate // n
+    owners = n // 2
+    first = n // 4
+    own = gate // owners
 
     def gather(value, bits):
         out = 0
@@ -118,6 +120,39 @@
             return carry
 
         lax.fori_loop(1, count, step, 0)
+
+    quarter = n // 4
+    column = lax.div(slot, quarter)
+    upper = lax.div(column, 2)
+    inner = column + upper * (3 - 2 * column)
+
+    def far_first(fn):
+        for rank, place in enumerate((3, 2, 1 - inner, inner)):
+            base = (place + upper * (3 - 2 * place)) * quarter
+
+            def step(k, carry):
+                fn(base + lax.rem(slot + 1 + k, quarter))
+                return carry
+
+            lax.fori_loop(0, quarter - (rank == 3), step, 0)
+
+    def owners_far_first(fn):
+        for rank in range(2):
+            base = (2 - rank + upper * (2 * rank - 1)) * quarter
+
+            def step(k, carry):
+                fn(base + lax.rem(slot + 1 + k, quarter))
+                return carry
+
+            lax.fori_loop(0, quarter - rank, step, 0)
+
+            if rank == 1:
+
+                @pl.when(jnp.logical_not(is_owner))
+                def _():
+                    fn(base + lax.rem(slot, quarter))
+
+    is_owner = inner == 1
 
     def remote(src, dst, phase, there, here, target):
         return pltpu.make_async_remote_copy(
@@ -133,7 +168,7 @@
         return ref.at[:, pl.ds(pl.multiple_of(j * size, size), size), :]
 
     def send_all(src, dst, phase, size):
-        others(lambda j: remote(block(src, j, size), block(dst, slot, size), phase, j, slot, peer(j)).start())
+        far_first(lambda j: remote(block(src, j, size), block(dst, slot, size), phase, j, slot, peer(j)).start())
 
     def recv_all(dst, phase, size):
         others(lambda j: remote(block(dst, j, size), block(dst, j, size), phase, j, j, peer(j)).wait_recv())
@@ -184,42 +219,51 @@
         outer = dot3((phi_t[0], phi_t[1]), state, ((1,), (0,)))
         part[s, 0] = outer[:gate, :gate] + outer[gate:, gate:]
         part[s, 1] = outer[gate:, :gate] - outer[:gate, gate:]
-        others(
-            lambda j: remote(block(part.at[s], j, own), rs_buf.at[s, slot], RS + s, j, slot, peer(j)).start()
+        owners_far_first(
+            lambda j: remote(block(part.at[s], j - first, own), rs_buf.at[s, slot], RS + s, j, slot, peer(j)).start()
         )
         if s + 1 < SECTIONS:
             phi = advance_adjoint(swap(phi, order[s + 1], per), s + 1)
-        others(
-            lambda j: remote(rs_buf.at[s, j], rs_buf.at[s, j], RS + s, j, j, peer(j)).wait_recv()
-        )
-        mine = pl.ds(pl.multiple_of(slot * own, own), own)
-        rs_buf[s, slot] = part[s, :, mine, :]
-        total = rs_buf[s, 0]
-        for j in range(1, n):
-            total = total + rs_buf[s, j]
-        if extra > 1:
-            mid_buf[s, layer] = total
+
+        @pl.when(is_owner)
+        def _():
+            mine = pl.ds(pl.multiple_of((slot - first) * own, own), own)
             others(
-                lambda j: remote(mid_buf.at[s, layer], mid_buf.at[s, layer], MID + s, j, layer, layer_peer(j)).start(),
-                layer, extra,
+                lambda j: remote(rs_buf.at[s, j], rs_buf.at[s, j], RS + s, j, j, peer(j)).wait_recv()
             )
-            others(
-                lambda j: remote(mid_buf.at[s, j], mid_buf.at[s, j], MID + s, j, j, layer_peer(j)).wait_recv(),
-                layer, extra,
-            )
-            total = mid_buf[s, 0]
-            for j in range(1, extra):
-                total = total + mid_buf[s, j]
-        ag_buf[s, :, mine, :] = total
-        held = block(ag_buf.at[s], slot, own)
-        others(lambda j: remote(held, held, AG + s, j, slot, peer(j)).start())
+            rs_buf[s, slot] = part[s, :, mine, :]
+            total = rs_buf[s, 0]
+            for j in range(1, n):
+                total = total + rs_buf[s, j]
+            if extra > 1:
+                mid_buf[s, layer] = total
+                others(
+                    lambda j: remote(mid_buf.at[s, layer], mid_buf.at[s, layer], MID + s, j, layer, layer_peer(j)).start(),
+                    layer, extra,
+                )
+                others(
+                    lambda j: remote(mid_buf.at[s, j], mid_buf.at[s, j], MID + s, j, j, layer_peer(j)).wait_recv(),
+                    layer, extra,
+                )
+                total = mid_buf[s, 0]
+                for j in range(1, extra):
+                    total = total + mid_buf[s, j]
+            ag_buf[s, :, mine, :] = total
+            held = block(ag_buf.at[s], slot - first, own)
+            far_first(lambda j: remote(held, held, AG + s, j, slot, peer(j)).start())
+
         if s + 2 == SECTIONS:
             back = phi
             for q in order[::-1]:
                 back = swap(back, q, per)
             adj_send[0] = back[:, :gate]
             adj_send[1] = back[:, gate:]
-        recv_all(ag_buf.at[s], AG + s, own)
+
+        def arrive(j):
+            held = block(ag_buf.at[s], j - first, own)
+            remote(held, held, AG + s, j, j, peer(j)).wait_recv()
+
+        owners_far_first(arrive)
         if s + 2 == SECTIONS:
             send_all(adj_send, adj_out, ADJ_OUT, per)
         fitted = polar(jnp.concatenate([ag_buf[s, 0], ag_buf[s, 1]], axis=1), NS_ITERS)
@@ -240,13 +284,23 @@
     sent_all(adj_in, ADJ_IN, per)
     sent_all(psi_in, PSI_IN, per)
     for s in range(SECTIONS):
-        sent_all(part.at[s], RS + s, own)
-        sent_all(ag_buf.at[s], AG + s, own)
-        if extra > 1:
-            others(
-                lambda j: remote(mid_buf.at[s, layer], mid_buf.at[s, layer], MID + s, j, j, layer_peer(j)).wait_send(),
-                layer, extra,
-            )
+
+        def left(j):
+            held = block(part.at[s], j - first, own)
+            remote(held, held, RS + s, j, j, peer(j)).wait_send()
+
+        owners_far_first(left)
+
+        @pl.when(is_owner)
+        def _():
+            held = block(ag_buf.at[s], slot - first, own)
+            others(lambda j: remote(held, held, AG + s, j, j, peer(j)).wait_send())
+            if extra > 1:
+                others(
+                    lambda j: remote(mid_buf.at[s, layer], mid_buf.at[s, layer], MID + s, j, j, layer_peer(j)).wait_send(),
+                    layer, extra,
+                )
+
     sent_all(adj_send, ADJ_OUT, per)
     recv_all(adj_out, ADJ_OUT, per)
     adj_back.wait()
@@ -264,7 +318,7 @@
     extra_bits = [bit for bit in range(bit_count) if bit not in used]
     n, extra = 2 ** len(used), 2 ** len(extra_bits)
     planes, rows, gate = initial_state.shape
-    own = gate // n
+    own = gate // (n // 2)
     f32, bf16 = jnp.float32, jnp.bfloat16
     anywhere = pl.BlockSpec(memory_space=pl.ANY)
     return tuple(

time: 94 us -> 93.8 us (level)
  no operation moved by 1% of the time
where the time goes in v2:
time: 93.8 us; the launch traced here: 93.7 us
  Pallas kernels  90.6 us (97%)
  local copies, waits for them, and re-layouts  2.42 us (3%)
    pallas_call x1, Pallas kernels, shards(): pl.pallas_call(functools.partial(kernel, used, order, extra_bits), out_sh...  90.6 us
    unnamed x4, local copies, waits for them, and re-layouts  2.42 us

profile of v2, /device:TPU:0, one launch (start us, length us, event | category | flops | bytes accessed | tf_op | source)
XLA Modules:
  0.0 93.7 jit_solution(9119149716652050796)
XLA Ops:
  0.6 90.6 %sweep.1 = (f32[2,256,128]{2,1,0:T(8,128)}, f32[2,256,128]{2,1,0:T(8,128)}) custom-call(f32[2,256,128]{2,1,0:T(8,128)} %psi_in.1, f32[2,256,128]{2,1,0:T(8,128)} %adj_in.1, f32[4,2,128,128]{3,2,1,0:T(8,128)} %gates_in.1), custom_call_target="tpu_custom_call" | custom-call | tf_op jit(solution)/shard_map/sweep/pallas_call | solution.py:325
  91.2 0.0 copy-start
  91.3 1.7 %copy.7 = f32[2,256,128]{2,1,0:T(8,128)} copy(f32[2,256,128]{2,1,0:T(8,128)} %get-tuple-element.4) | data formatting | bytes 524288
  93.0 0.0 copy-done
  93.0 0.7 copy.8
Async XLA Ops:
  91.2 1.7 %copy-start = (f32[2,256,128]{2,1,0:T(8,128)S(1)}, f32[2,256,128]{2,1,0:T(8,128)}, u32[]{:S(2)}) copy-start(f32[2,256,128]{2,1,0:T(8,128)} %get-tuple-element.5) | copy-start | bytes 786436

commit v3 on v2

v3 whole, which is shorter than its diff:
```python
import functools

import jax
import jax.numpy as jnp
from jax import lax
from jax.experimental import pallas as pl
from jax.experimental.pallas import tpu as pltpu
from jax.sharding import PartitionSpec as P

SECTIONS = 4
NS_ITERS = 8
MESH = pl.DeviceIdType.MESH
ADJ_IN, PSI_IN, RS, AG, MID, ADJ_OUT, PSI_OUT = 0, 1, 2, 6, 10, 14, 15


def split(x):
    high = x.astype(jnp.bfloat16)
    return high, (x - high.astype(jnp.float32)).astype(jnp.bfloat16)


def dot3(left, right, contract):
    def dot(a, b):
        return lax.dot_general(
            a, b, (contract, ((), ())), preferred_element_type=jnp.float32
        )

    return dot(left[0], right[0]) + (dot(left[0], right[1]) + dot(left[1], right[0]))


def embed_out(real, imag):
    return jnp.concatenate(
        [
            jnp.concatenate([real, -imag], axis=1),
            jnp.concatenate([imag, real], axis=1),
        ],
        axis=0,
    )


def swap_plane(plane, q, per):
    rows, lanes = plane.shape
    stride = per << q
    rolled = pltpu.roll(plane, lanes // 2, 1)
    low = lax.broadcasted_iota(jnp.int32, (stride, lanes), 1) < lanes // 2
    blocks = []
    for start in range(0, rows, 2 * stride):
        mid, end = start + stride, start + 2 * stride
        blocks.append(jnp.where(low, plane[start:mid], rolled[mid:end]))
        blocks.append(jnp.where(low, rolled[start:mid], plane[mid:end]))
    return jnp.concatenate(blocks, axis=0)


def swap(x, q, per):
    lanes = x.shape[1] // 2
    return jnp.concatenate(
        [swap_plane(x[:, :lanes], q, per), swap_plane(x[:, lanes:], q, per)], axis=1
    )


def polar(x, sweeps):
    gate = x.shape[0]
    norm = lax.rsqrt(jnp.sum(x * x, keepdims=True) + 1e-06)

    def sweep(_, a):
        high, low = split(a)

        def embed(v):
            real, imag = v[:, :gate], v[:, gate:]
            return jnp.concatenate([v, jnp.concatenate([-imag, real], axis=1)], axis=0)

        full = (embed(high), embed(low))
        def product(left, axis):
            def dot(u, v):
                return lax.dot_general(
                    u, v, (((1,), (axis,)), ((), ())), preferred_element_type=jnp.float32
                )

            both = dot(jnp.concatenate(left, axis=0), full[0])
            return both[:gate] + (both[gate:] + dot(left[0], full[1]))

        gram = product((high, low), 1)
        return 1.5 * a - 0.5 * product(split(gram), 0)

    return lax.fori_loop(0, sweeps, sweep, x * norm)


def kernel(
    used, order, extra_bits,
    psi_in, adj_in, gates_in, psi_out, adj_out,
    psi_buf, adj_buf, gates, phi_t, psi_send, adj_send,
    part, rs_buf, ag_buf, mid_buf,
    send_sem, recv_sem, local_sem,
):
    group = lax.axis_index("groups")
    me = lax.axis_index("long")
    n = 2 ** len(used)
    extra = 2 ** len(extra_bits)
    rows = psi_in.shape[1]
    gate = psi_in.shape[2]
    owners = n // 2
    first = n // 4
    own = gate // owners
    per = rows // owners

    def gather(value, bits):
        out = 0
        for k, bit in enumerate(bits):
            out = out + lax.rem(lax.div(value, 2**bit), 2) * 2**k
        return out

    def scatter(value, bits):
        out = 0
        for k, bit in enumerate(bits):
            out = out + lax.rem(lax.div(value, 2**k), 2) * 2**bit
        return out

    slot = gather(me, used)
    layer = gather(me, extra_bits)

    def peer(j):
        return scatter(j, used) + scatter(layer, extra_bits)

    def layer_peer(j):
        return scatter(slot, used) + scatter(j, extra_bits)

    def others(fn, mine=slot, count=n):
        def step(off, carry):
            fn(lax.rem(mine + off, count))
            return carry

        lax.fori_loop(1, count, step, 0)

    quarter = n // 4
    column = lax.div(slot, quarter)
    upper = lax.div(column, 2)
    inner = column + upper * (3 - 2 * column)

    def far_first(fn):
        for rank, place in enumerate((3, 2, 1 - inner, inner)):
            base = (place + upper * (3 - 2 * place)) * quarter

            def step(k, carry):
                fn(base + lax.rem(slot + 1 + k, quarter))
                return carry

            lax.fori_loop(0, quarter - (rank == 3), step, 0)

    def owners_far_first(fn, among=False):
        for rank in range(2):
            base = (2 - rank + upper * (2 * rank - 1)) * quarter

            def step(k, carry):
                fn(base + lax.rem(slot + 1 + k, quarter))
                return carry

            lax.fori_loop(0, quarter - rank, step, 0)

            if rank == 1 and not among:

                @pl.when(jnp.logical_not(is_owner))
                def _():
                    fn(base + lax.rem(slot, quarter))

    is_owner = inner == 1

    def remote(src, dst, phase, there, here, target):
        return pltpu.make_async_remote_copy(
            src_ref=src,
            dst_ref=dst,
            send_sem=send_sem.at[phase, there],
            recv_sem=recv_sem.at[phase, here],
            device_id={"groups": group, "long": target},
            device_id_type=MESH,
        )

    def block(ref, j, size):
        return ref.at[:, pl.ds(pl.multiple_of(j * size, size), size), :]

    index = slot - first

    def signal(j, target):
        pl.semaphore_signal(
            barrier, inc=1, device_id={"groups": group, "long": target(j)}, device_id_type=MESH
        )

    barrier = pltpu.get_barrier_semaphore()

    @pl.when(is_owner)
    def _():
        far_first(lambda j: signal(j, peer))
        if extra > 1:
            others(lambda j: signal(j, layer_peer), layer, extra)
        pl.semaphore_wait(barrier, n + extra - 2)

    @pl.when(jnp.logical_not(is_owner))
    def _():
        owners_far_first(lambda j: signal(j, peer))
        pl.semaphore_wait(barrier, owners)

    def inward(src, dst, phase):
        return lambda j: remote(
            block(src, j - first, per), block(dst, slot, per), phase, j, slot, peer(j)
        )

    def inward_from(dst, phase):
        return lambda j: remote(block(dst, j, per), block(dst, j, per), phase, j, j, peer(j))

    def outward(src, dst, phase):
        return lambda j: remote(
            block(src, j, per), block(dst, index, per), phase, j, slot, peer(j)
        )

    def outward_from(dst, phase):
        return lambda j: remote(
            block(dst, j - first, per), block(dst, j - first, per), phase, j, j, peer(j)
        )

    owners_far_first(lambda j: inward(adj_in, adj_buf, ADJ_IN)(j).start())
    owners_far_first(lambda j: inward(psi_in, psi_buf, PSI_IN)(j).start())

    def joined(ref):
        return jnp.concatenate([ref[0], ref[1]], axis=1)

    def put(ref, x):
        for q in order[::-1]:
            x = swap(x, q, per)
        ref[0] = x[:, :gate]
        ref[1] = x[:, gate:]

    def advance_adjoint(phi, s):
        full = split(embed_out(gates[s, 0], gates[s, 1]))
        phi = dot3(split(phi), full, ((1,), (1,)))
        high, low = split(phi.T)
        phi_t[0] = high
        phi_t[1] = low
        return phi

    @pl.when(is_owner)
    def _():
        gate_copy = pltpu.make_async_copy(gates_in, gates, local_sem.at[0])
        adj_own = pltpu.make_async_copy(block(adj_in, index, per), block(adj_buf, slot, per), local_sem.at[1])
        psi_own = pltpu.make_async_copy(block(psi_in, index, per), block(psi_buf, slot, per), local_sem.at[2])
        gate_copy.start()
        adj_own.start()
        psi_own.start()
        mine = pl.ds(pl.multiple_of(index * own, own), own)

        gate_copy.wait()
        adj_own.wait()
        others(lambda j: inward_from(adj_buf, ADJ_IN)(j).wait_recv())
        phi = advance_adjoint(swap(joined(adj_buf), order[0], per), 0)
        psi_own.wait()
        others(lambda j: inward_from(psi_buf, PSI_IN)(j).wait_recv())
        psi = swap(joined(psi_buf), order[0], per)

        for s in range(SECTIONS):
            state = split(psi)
            outer = dot3((phi_t[0], phi_t[1]), state, ((1,), (0,)))
            part[s, 0] = outer[:gate, :gate] + outer[gate:, gate:]
            part[s, 1] = outer[gate:, :gate] - outer[:gate, gate:]

            def to_owner(j):
                return remote(
                    block(part.at[s], j - first, own), rs_buf.at[s, index], RS + s, j, slot, peer(j)
                )

            def from_owner(j):
                held = rs_buf.at[s, j - first]
                return remote(held, held, RS + s, j, j, peer(j))

            owners_far_first(lambda j: to_owner(j).start(), True)
            if s + 1 < SECTIONS:
                phi = advance_adjoint(swap(phi, order[s + 1], per), s + 1)
            owners_far_first(lambda j: from_owner(j).wait_recv(), True)
            rs_buf[s, index] = part[s, :, mine, :]
            total = rs_buf[s, 0]
            for j in range(1, owners):
                total = total + rs_buf[s, j]
            if extra > 1:
                mid_buf[s, layer] = total

                def across(j, here):
                    held = mid_buf.at[s, here]
                    return remote(held, held, MID + s, j, here, layer_peer(j))

                others(lambda j: across(j, layer).start(), layer, extra)
                others(lambda j: across(j, j).wait_recv(), layer, extra)
                total = mid_buf[s, 0]
                for j in range(1, extra):
                    total = total + mid_buf[s, j]
            ag_buf[s, :, mine, :] = total
            held = block(ag_buf.at[s], index, own)
            owners_far_first(lambda j: remote(held, held, AG + s, j, slot, peer(j)).start(), True)
            if s + 2 == SECTIONS:
                put(adj_send, phi)

            def arrive(j):
                there = block(ag_buf.at[s], j - first, own)
                remote(there, there, AG + s, j, j, peer(j)).wait_recv()

            owners_far_first(arrive, True)
            if s + 2 == SECTIONS:
                far_first(lambda j: outward(adj_send, adj_out, ADJ_OUT)(j).start())
                adj_back = pltpu.make_async_copy(block(adj_send, slot, per), block(adj_out, index, per), local_sem.at[1])
                adj_back.start()
            fitted = polar(jnp.concatenate([ag_buf[s, 0], ag_buf[s, 1]], axis=1), NS_ITERS)
            full = split(embed_out(fitted[:, :gate], fitted[:, gate:]))
            psi = dot3(state, full, ((1,), (1,)))
            if s + 1 < SECTIONS:
                psi = swap(psi, order[s + 1], per)

        put(psi_send, psi)
        far_first(lambda j: outward(psi_send, psi_out, PSI_OUT)(j).start())
        psi_back = pltpu.make_async_copy(block(psi_send, slot, per), block(psi_out, index, per), local_sem.at[2])
        psi_back.start()
        for s in range(SECTIONS):
            owners_far_first(
                lambda j: remote(block(part.at[s], j - first, own), rs_buf.at[s, index], RS + s, j, slot, peer(j)).wait_send(),
                True,
            )
            sent = block(ag_buf.at[s], index, own)
            owners_far_first(lambda j: remote(sent, sent, AG + s, j, slot, peer(j)).wait_send(), True)
            if extra > 1:
                done = mid_buf.at[s, layer]
                others(lambda j: remote(done, done, MID + s, j, layer, layer_peer(j)).wait_send(), layer, extra)
        adj_back.wait()
        psi_back.wait()
        others(lambda j: outward(adj_send, adj_out, ADJ_OUT)(j).wait_send())
        others(lambda j: outward(psi_send, psi_out, PSI_OUT)(j).wait_send())

    owners_far_first(lambda j: inward(adj_in, adj_buf, ADJ_IN)(j).wait_send())
    owners_far_first(lambda j: inward(psi_in, psi_buf, PSI_IN)(j).wait_send())
    owners_far_first(lambda j: outward_from(adj_out, ADJ_OUT)(j).wait_recv())
    owners_far_first(lambda j: outward_from(psi_out, PSI_OUT)(j).wait_recv())


def shards(initial_state, adjoint_state, current_gates):
    bit_count = lax.axis_size("long").bit_length() - 1
    partner_bits = [bit_count - 1, bit_count // 2, 0, 1]
    used = sorted(set(partner_bits))
    assert len(used) == SECTIONS
    order = [used.index(bit) for bit in partner_bits]
    extra_bits = [bit for bit in range(bit_count) if bit not in used]
    n, extra = 2 ** len(used), 2 ** len(extra_bits)
    planes, rows, gate = initial_state.shape
    owners = n // 2
    own = gate // owners
    held = n * (rows // owners)
    f32, bf16 = jnp.float32, jnp.bfloat16
    anywhere = pl.BlockSpec(memory_space=pl.ANY)
    return tuple(
        pl.pallas_call(
            functools.partial(kernel, used, order, extra_bits),
            out_shape=[jax.ShapeDtypeStruct(initial_state.shape, f32)] * 2,
            in_specs=[anywhere] * 3,
            out_specs=[anywhere] * 2,
            scratch_shapes=[
                pltpu.VMEM((2, held, gate), f32),
                pltpu.VMEM((2, held, gate), f32),
                pltpu.VMEM(current_gates.shape, f32),
                pltpu.VMEM((2, 2 * gate, held), bf16),
                pltpu.VMEM((2, held, gate), f32),
                pltpu.VMEM((2, held, gate), f32),
                pltpu.VMEM((SECTIONS, 2, gate, gate), f32),
                pltpu.VMEM((SECTIONS, owners, 2, own, gate), f32),
                pltpu.VMEM((SECTIONS, 2, gate, gate), f32),
                pltpu.VMEM((SECTIONS, extra, 2, own, gate), f32),
                pltpu.SemaphoreType.DMA((16, max(n, extra))),
                pltpu.SemaphoreType.DMA((16, max(n, extra))),
                pltpu.SemaphoreType.DMA((3,)),
            ],
            compiler_params=pltpu.CompilerParams(collective_id=0, has_side_effects=True),
            name="sweep",
        )(initial_state, adjoint_state, current_gates)
    )


def solution(mesh):
    return jax.shard_map(
        shards,
        mesh=mesh,
        in_specs=(
            P(None, ("groups", "long"), None),
            P(None, ("groups", "long"), None),
            P("groups", None, None, None),
        ),
        out_specs=(P(None, ("groups", "long"), None), P(None, ("groups", "long"), None)),
        check_vma=False,
    )
```

time: 93.8 us -> 83.9 us (0.89)
  Pallas kernels: 90.6 us -> 80.7 us
    pallas_call x1, Pallas kernels: 90.6 us -> 80.7 us  [shards(): pl.pallas_call(functools.partial(kernel, used, order, extra_bits), out_sh...]
where the time goes in v3:
time: 83.9 us; the launch traced here: 83.7 us
  Pallas kernels  80.7 us (96%)
  local copies, waits for them, and re-layouts  2.42 us (3%)
    pallas_call x1, Pallas kernels, shards(): pl.pallas_call(functools.partial(kernel, used, order, extra_bits), out_sh...  80.7 us
    unnamed x4, local copies, waits for them, and re-layouts  2.42 us

profile of v3, /device:TPU:0, one launch (start us, length us, event | category | flops | bytes accessed | tf_op | source)
XLA Modules:
  0.0 83.7 jit_solution(6006383784910041008)
XLA Ops:
  0.6 80.7 %sweep.1 = (f32[2,256,128]{2,1,0:T(8,128)}, f32[2,256,128]{2,1,0:T(8,128)}) custom-call(f32[2,256,128]{2,1,0:T(8,128)} %psi_in.1, f32[2,256,128]{2,1,0:T(8,128)} %adj_in.1, f32[4,2,128,128]{3,2,1,0:T(8,128)} %gates_in.1), custom_call_target="tpu_custom_call" | custom-call | tf_op jit(solution)/shard_map/sweep/pallas_call | solution.py:352
  81.3 0.0 copy-start
  81.3 1.7 %copy.7 = f32[2,256,128]{2,1,0:T(8,128)} copy(f32[2,256,128]{2,1,0:T(8,128)} %get-tuple-element.4) | data formatting | bytes 524288
  83.0 0.0 copy-done
  83.0 0.7 copy.8
Async XLA Ops:
  81.3 1.7 %copy-start = (f32[2,256,128]{2,1,0:T(8,128)S(1)}, f32[2,256,128]{2,1,0:T(8,128)}, u32[]{:S(2)}) copy-start(f32[2,256,128]{2,1,0:T(8,128)} %get-tuple-element.5) | copy-start | bytes 786436

commit v4 on v3

--- a/solution.py
+++ b/solution.py
@@ -135,8 +135,9 @@
     upper = lax.div(column, 2)
     inner = column + upper * (3 - 2 * column)
 
-    def far_first(fn):
-        for rank, place in enumerate((3, 2, 1 - inner, inner)):
+    def far_first(fn, ranks=(0, 1, 2, 3)):
+        for rank in ranks:
+            place = (3, 2, 1 - inner, inner)[rank]
             base = (place + upper * (3 - 2 * place)) * quarter
 
             def step(k, carry):
@@ -231,8 +232,8 @@
         full = split(embed_out(gates[s, 0], gates[s, 1]))
         phi = dot3(split(phi), full, ((1,), (1,)))
         high, low = split(phi.T)
-        phi_t[0] = high
-        phi_t[1] = low
+        phi_t[s, 0] = high
+        phi_t[s, 1] = low
         return phi
 
     @pl.when(is_owner)
@@ -248,14 +249,19 @@
         gate_copy.wait()
         adj_own.wait()
         others(lambda j: inward_from(adj_buf, ADJ_IN)(j).wait_recv())
-        phi = advance_adjoint(swap(joined(adj_buf), order[0], per), 0)
+        phi = joined(adj_buf)
+        for s in range(SECTIONS):
+            phi = advance_adjoint(swap(phi, order[s], per), s)
+        put(adj_send, phi)
+        adj_back = pltpu.make_async_copy(block(adj_send, slot, per), block(adj_out, index, per), local_sem.at[1])
+        adj_back.start()
         psi_own.wait()
         others(lambda j: inward_from(psi_buf, PSI_IN)(j).wait_recv())
         psi = swap(joined(psi_buf), order[0], per)
 
         for s in range(SECTIONS):
             state = split(psi)
-            outer = dot3((phi_t[0], phi_t[1]), state, ((1,), (0,)))
+            outer = dot3((phi_t[s, 0], phi_t[s, 1]), state, ((1,), (0,)))
             part[s, 0] = outer[:gate, :gate] + outer[gate:, gate:]
             part[s, 1] = outer[gate:, :gate] - outer[:gate, gate:]
 
@@ -269,8 +275,6 @@
                 return remote(held, held, RS + s, j, j, peer(j))
 
             owners_far_first(lambda j: to_owner(j).start(), True)
-            if s + 1 < SECTIONS:
-                phi = advance_adjoint(swap(phi, order[s + 1], per), s + 1)
             owners_far_first(lambda j: from_owner(j).wait_recv(), True)
             rs_buf[s, index] = part[s, :, mine, :]
             total = rs_buf[s, 0]
@@ -291,18 +295,15 @@
             ag_buf[s, :, mine, :] = total
             held = block(ag_buf.at[s], index, own)
             owners_far_first(lambda j: remote(held, held, AG + s, j, slot, peer(j)).start(), True)
-            if s + 2 == SECTIONS:
-                put(adj_send, phi)
 
             def arrive(j):
                 there = block(ag_buf.at[s], j - first, own)
                 remote(there, there, AG + s, j, j, peer(j)).wait_recv()
 
             owners_far_first(arrive, True)
-            if s + 2 == SECTIONS:
-                far_first(lambda j: outward(adj_send, adj_out, ADJ_OUT)(j).start())
-                adj_back = pltpu.make_async_copy(block(adj_send, slot, per), block(adj_out, index, per), local_sem.at[1])
-                adj_back.start()
+            if s < 3:
+                back_ranks = ((2, 3), (0,), (1,))[s]
+                far_first(lambda j: outward(adj_send, adj_out, ADJ_OUT)(j).start(), back_ranks)
             fitted = polar(jnp.concatenate([ag_buf[s, 0], ag_buf[s, 1]], axis=1), NS_ITERS)
             full = split(embed_out(fitted[:, :gate], fitted[:, gate:]))
             psi = dot3(state, full, ((1,), (1,)))
@@ -358,7 +359,7 @@
                 pltpu.VMEM((2, held, gate), f32),
                 pltpu.VMEM((2, held, gate), f32),
                 pltpu.VMEM(current_gates.shape, f32),
-                pltpu.VMEM((2, 2 * gate, held), bf16),
+                pltpu.VMEM((SECTIONS, 2, 2 * gate, held), bf16),
                 pltpu.VMEM((2, held, gate), f32),
                 pltpu.VMEM((2, held, gate), f32),
                 pltpu.VMEM((SECTIONS, 2, gate, gate), f32),

time: 83.9 us -> 83.4 us (level)
  no operation moved by 1% of the time
where the time goes in v4:
time: 83.4 us; the launch traced here: 83.3 us
  Pallas kernels  80.2 us (96%)
  local copies, waits for them, and re-layouts  2.42 us (3%)
    pallas_call x1, Pallas kernels, shards(): pl.pallas_call(functools.partial(kernel, used, order, extra_bits), out_sh...  80.2 us
    unnamed x4, local copies, waits for them, and re-layouts  2.42 us

profile of v4, /device:TPU:0, one launch (start us, length us, event | category | flops | bytes accessed | tf_op | source)
XLA Modules:
  0.0 83.3 jit_solution(9723491699995240732)
XLA Ops:
  0.6 80.2 %sweep.1 = (f32[2,256,128]{2,1,0:T(8,128)}, f32[2,256,128]{2,1,0:T(8,128)}) custom-call(f32[2,256,128]{2,1,0:T(8,128)} %psi_in.1, f32[2,256,128]{2,1,0:T(8,128)} %adj_in.1, f32[4,2,128,128]{3,2,1,0:T(8,128)} %gates_in.1), custom_call_target="tpu_custom_call" | custom-call | tf_op jit(solution)/shard_map/sweep/pallas_call | solution.py:353
  80.8 0.0 copy-start
  80.8 1.7 %copy.7 = f32[2,256,128]{2,1,0:T(8,128)} copy(f32[2,256,128]{2,1,0:T(8,128)} %get-tuple-element.4) | data formatting | bytes 524288
  82.5 0.0 copy-done
  82.6 0.7 copy.8
Async XLA Ops:
  80.8 1.7 %copy-start = (f32[2,256,128]{2,1,0:T(8,128)S(1)}, f32[2,256,128]{2,1,0:T(8,128)}, u32[]{:S(2)}) copy-start(f32[2,256,128]{2,1,0:T(8,128)} %get-tuple-element.5) | copy-start | bytes 786436

commit v5 on v4

--- a/solution.py
+++ b/solution.py
@@ -81,7 +81,7 @@
         gram = product((high, low), 1)
         return 1.5 * a - 0.5 * product(split(gram), 0)
 
-    return lax.fori_loop(0, sweeps, sweep, x * norm)
+    return lax.fori_loop(0, sweeps, sweep, x * norm, unroll=8)
 
 
 def kernel(
@@ -352,9 +352,9 @@
     return tuple(
         pl.pallas_call(
             functools.partial(kernel, used, order, extra_bits),
-            out_shape=[jax.ShapeDtypeStruct(initial_state.shape, f32)] * 2,
+            out_shape=[pltpu.VMEM(initial_state.shape, f32)] * 2,
             in_specs=[anywhere] * 3,
-            out_specs=[anywhere] * 2,
+            out_specs=[pl.BlockSpec(memory_space=pltpu.VMEM)] * 2,
             scratch_shapes=[
                 pltpu.VMEM((2, held, gate), f32),
                 pltpu.VMEM((2, held, gate), f32),

time: 83.4 us -> 81.5 us (0.977)
  local copies, waits for them, and re-layouts: 2.42 us -> 1.41 us
  Pallas kernels: 80.2 us -> 79.3 us
    unnamed x4 -> x2, local copies, waits for them, and re-layouts: 2.42 us -> 1.41 us
    pallas_call x1, Pallas kernels: 80.2 us -> 79.3 us  [shards(): pl.pallas_call(functools.partial(kernel, used, order, extra_bits), out_sh...]
where the time goes in v5:
time: 81.5 us; the launch traced here: 81.3 us
  Pallas kernels  79.3 us (97%)
  local copies, waits for them, and re-layouts  1.41 us (2%)
    pallas_call x1, Pallas kernels, shards(): pl.pallas_call(functools.partial(kernel, used, order, extra_bits), out_sh...  79.3 us

profile of v5, /device:TPU:0, one launch (start us, length us, event | category | flops | bytes accessed | tf_op | source)
XLA Modules:
  0.0 81.3 jit_solution(6341042193951143273)
XLA Ops:
  0.6 79.3 %sweep.1 = (f32[2,256,128]{2,1,0:T(8,128)S(1)}, f32[2,256,128]{2,1,0:T(8,128)S(1)}) custom-call(f32[2,256,128]{2,1,0:T(8,128)} %psi_in.1, f32[2,256,128]{2,1,0:T(8,128)} %adj_in.1, f32[4,2,128,128]{3,2,1,0:T(8,128)} %gates_in.1), custom_call_target="tpu_custom_call" | custom-call | tf_op jit(solution)/shard_map/sweep/pallas_call | solution.py:353
  79.9 0.7 copy.7
  80.6 0.7 copy.8
